TPU v7x, 32 devices: a whole 2x2x4 slice. The times are simulated.
32 devices in a mesh: gx: 4 (over z), gy: 8 (over y, x, core).
Axes of the slice: x: 2, y: 2, z: 4, core: 2. Of those that a mesh axis runs over, the one named last changes fastest.
Arguments:
- right_side: float32 [2048, 4096], P('gx', 'gy'), may hold values from -8 to 8
- drift_x: float32 [2048, 4096], P('gx', 'gy'), may hold values from -0.9 to 0.9
- drift_y: float32 [2048, 4096], P('gx', 'gy'), may hold values from -0.9 to 0.9
- sketch_rows: float32 [256, 2048], P(None, 'gx'), may hold values from -0.375 to 0.375
- sketch_cols: float32 [256, 4096], P(None, 'gy'), may hold values from -6 to 6
Outputs:
- solution: float32 [2048, 4096], P('gx', 'gy')
- residual: float32 [2048, 4096], P('gx', 'gy')
All inputs are finite; a program needn't handle non-finite values.
Results may differ from a plain program's by a relative error of at most 0.0003.
Values sent between devices are 32-bit elements; how exact they have to be, the bound alone decides.
A program may use at most 64 MiB of HBM per device.

v0:
```python
import jax
import jax.numpy as jnp
from jax import lax
from jax.sharding import PartitionSpec as P

ITERS = 4
shift_value = 0.05


def padded_2(cells, sides, width):
    for axis, dim in sides:
        count = lax.axis_size(axis)
        ends = count - 1
        head = lax.slice_in_dim(cells, 0, width, axis=dim)
        tail = lax.slice_in_dim(cells, cells.shape[dim] - width, cells.shape[dim], axis=dim)
        cells = jnp.concatenate(
            [
                lax.ppermute(tail, axis, [(i, (i + 1) % count) for i in range(ends)]),
                cells,
                lax.ppermute(head, axis, [((i + 1) % count, i) for i in range(ends)]),
            ],
            axis=dim,
        )
    return cells


def stencil(padded, field, drift_x, drift_y):
    upper_cells = padded[:-2, 1:-1]
    lower_cells = padded[2:, 1:-1]
    left_cells = padded[1:-1, :-2]
    right_cells = padded[1:-1, 2:]
    return (
        (4.0 + shift_value) * field
        - (1.0 + drift_x) * upper_cells
        - (1.0 - drift_x) * lower_cells
        - (1.0 + drift_y) * left_cells
        - (1.0 - drift_y) * right_cells
    )


def solve_small(hessenberg, beta_norm):
    gram_matrix = jnp.dot(hessenberg.T, hessenberg, precision=lax.Precision.HIGHEST)
    target = beta_norm * hessenberg[0]
    factor = jnp.linalg.cholesky(gram_matrix)
    count = hessenberg.shape[1]
    forward = []
    for row in range(count):
        acc = target[row]
        for col in range(row):
            acc = acc - factor[row, col] * forward[col]
        forward.append(acc / factor[row, row])
    backward = [None] * count
    for row in reversed(range(count)):
        acc = forward[row]
        for col in range(row + 1, count):
            acc = acc - factor[col, row] * backward[col]
        backward[row] = acc / factor[row, row]
    return backward


def body(right_side, drift_x, drift_y, sketch_rows, sketch_cols):

    def sketch(field):
        product = jnp.dot(field, sketch_cols.T, precision=lax.Precision.HIGHEST)
        partial_value = jnp.einsum(
            "ki,ik->k", sketch_rows, product, precision=lax.Precision.HIGHEST
        )
        return lax.psum(partial_value, ("gx", "gy"))

    first_sketch = sketch(right_side)
    beta_norm = jnp.sqrt(jnp.sum(first_sketch * first_sketch))
    basis_vectors = [right_side / beta_norm]
    sketched = [first_sketch / beta_norm]
    images = []
    columns = []
    for column in range(ITERS):
        current = basis_vectors[column]
        padded = padded_2(current, (("gx", 0), ("gy", 1)), 1)
        applied = stencil(padded, current, drift_x, drift_y)
        images.append(applied)
        sketch_image = sketch(applied)
        sketch_matrix = jnp.stack(sketched, axis=1)
        projection = jnp.dot(sketch_matrix.T, sketch_image, precision=lax.Precision.HIGHEST)
        remainder = applied
        for index_prev in range(column + 1):
            remainder = remainder - projection[index_prev] * basis_vectors[index_prev]
        remainder_sketch = sketch_image - jnp.dot(
            sketch_matrix, projection, precision=lax.Precision.HIGHEST
        )
        new_norm = jnp.sqrt(jnp.sum(remainder_sketch * remainder_sketch))
        basis_vectors.append(remainder / new_norm)
        sketched.append(remainder_sketch / new_norm)
        entries = jnp.concatenate(
            [projection, new_norm[None], jnp.zeros((ITERS - column - 1,), jnp.float32)]
        )
        columns.append(entries)
    hessenberg = jnp.stack(columns, axis=1)
    coeffs = solve_small(hessenberg, beta_norm)
    solution = jnp.zeros_like(right_side)
    for column in range(ITERS):
        solution = solution + coeffs[column] * basis_vectors[column]
    padded = padded_2(solution, (("gx", 0), ("gy", 1)), 1)
    residual = right_side - stencil(padded, solution, drift_x, drift_y)
    return (solution, residual)


def solution(mesh):
    in_specs = (P("gx", "gy"), P("gx", "gy"), P("gx", "gy"), P(None, "gx"), P(None, "gy"))
    out_specs = (P("gx", "gy"), P("gx", "gy"))
    return jax.shard_map(body, mesh=mesh, in_specs=in_specs, out_specs=out_specs, check_vma=False)
```

profile of v0, /device:TPU:1, one launch (start us, length us, event | category | flops | bytes accessed | tf_op | source)
XLA Modules:
  0.0 370.7 jit_solution(15757160799951034432)
XLA Ops:
  1.7 2.3 convolution_bitcast_fusion.4
  4.3 40.5 %psum.35 = f32[256]{0:T(256)S(1)} all-reduce(f32[256]{0:T(256)S(1)} %multiply_reduce_fusion.4), channel_id=1, replica_groups=mesh['gx'=4,'gy'=8] {'gx','gy'}, use_global_device_ids=true, to_apply=%region_0.0 | all-reduce | flops 256 | bytes 2048 | tf_op jit(solution)/shard_map/psum | solution.py:68
  46.3 3.3 collective-permute-start
  50.9 3.0 collective-permute-done.1
  54.1 6.7 %collective-permute-start.2 = (f32[514,1]{1,0:T(8,128)S(1)}, f32[514,1]{1,0:T(8,128)S(1)}, u32[]{:S(2)}, u32[]{:S(2)}) collective-permute-start(f32[514,1]{1,0:T(8,128)S(1)} %get-tuple-element.16), channel_id=1, source_target_pairs={{0,1},{1,2},{2,3},{3,4},{4,5},{5,6},{6,7},{8,9},{9,10},{10,11},{11... | collective-permute-start | bytes 6176 | tf_op jit(solution)/shard_map/ppermute | solution.py:18
  64.1 4.5 %collective-permute-done.3 = f32[514,1]{1,0:T(8,128)S(1)} collective-permute-done((f32[514,1]{1,0:T(8,128)S(1)}, f32[514,1]{1,0:T(8,128)S(1)}, u32[]{:S(2)}, u32[]{:S(2)}) %collective-permute-start.3) | collective-permute-done | bytes 2088 | tf_op jit(solution)/shard_map/ppermute | solution.py:20
  71.8 38.4 %psum.36 = f32[256]{0:T(256)S(1)} all-reduce(f32[256]{0:T(256)S(1)} %multiply_reduce_fusion.3), channel_id=1, replica_groups=mesh['gx'=4,'gy'=8] {'gx','gy'}, use_global_device_ids=true, to_apply=%region_2.0 | all-reduce | flops 256 | bytes 2048 | tf_op jit(solution)/shard_map/psum | solution.py:68
  112.8 2.2 subtract_divide_fusion.2
  115.0 2.4 collective-permute-start.4
  119.3 2.4 collective-permute-done.5
  121.8 6.7 %collective-permute-start.6 = (f32[514,1]{1,0:T(8,128)S(1)}, f32[514,1]{1,0:T(8,128)S(1)}, u32[]{:S(2)}, u32[]{:S(2)}) collective-permute-start(f32[514,1]{1,0:T(8,128)S(1)} %get-tuple-element.14), channel_id=1, source_target_pairs={{0,1},{1,2},{2,3},{3,4},{4,5},{5,6},{6,7},{8,9},{9,10},{10,11},{11... | collective-permute-start | bytes 6176 | tf_op jit(solution)/shard_map/ppermute | solution.py:18
  131.9 4.5 %collective-permute-done.7 = f32[514,1]{1,0:T(8,128)S(1)} collective-permute-done((f32[514,1]{1,0:T(8,128)S(1)}, f32[514,1]{1,0:T(8,128)S(1)}, u32[]{:S(2)}, u32[]{:S(2)}) %collective-permute-start.7) | collective-permute-done | bytes 2088 | tf_op jit(solution)/shard_map/ppermute | solution.py:20
  143.2 37.7 %psum.37 = f32[256]{0:T(256)S(1)} all-reduce(f32[256]{0:T(256)S(1)} %multiply_reduce_fusion.2), channel_id=1, replica_groups=mesh['gx'=4,'gy'=8] {'gx','gy'}, use_global_device_ids=true, to_apply=%region_4.0 | all-reduce | flops 256 | bytes 2048 | tf_op jit(solution)/shard_map/psum | solution.py:68
  183.1 2.9 subtract_divide_fusion.1
  186.0 3.1 collective-permute-start.8
  190.5 3.0 collective-permute-done.9
  193.6 6.7 %collective-permute-start.10 = (f32[514,1]{1,0:T(8,128)S(1)}, f32[514,1]{1,0:T(8,128)S(1)}, u32[]{:S(2)}, u32[]{:S(2)}) collective-permute-start(f32[514,1]{1,0:T(8,128)S(1)} %get-tuple-element.12), channel_id=1, source_target_pairs={{0,1},{1,2},{2,3},{3,4},{4,5},{5,6},{6,7},{8,9},{9,10},{10,11},{11... | collective-permute-start | bytes 6176 | tf_op jit(solution)/shard_map/ppermute | solution.py:18
  200.3 2.1 collective-permute-start.11
  203.7 4.5 %collective-permute-done.11 = f32[514,1]{1,0:T(8,128)S(1)} collective-permute-done((f32[514,1]{1,0:T(8,128)S(1)}, f32[514,1]{1,0:T(8,128)S(1)}, u32[]{:S(2)}, u32[]{:S(2)}) %collective-permute-start.11) | collective-permute-done | bytes 2088 | tf_op jit(solution)/shard_map/ppermute | solution.py:20
  215.0 37.8 %psum.38 = f32[256]{0:T(256)S(1)} all-reduce(f32[256]{0:T(256)S(1)} %multiply_reduce_fusion.1), channel_id=1, replica_groups=mesh['gx'=4,'gy'=8] {'gx','gy'}, use_global_device_ids=true, to_apply=%region_6.0 | all-reduce | flops 256 | bytes 2048 | tf_op jit(solution)/shard_map/psum | solution.py:68
  254.9 3.9 %subtract_divide_fusion = f32[512,512]{1,0:T(8,128)S(1)} fusion(f32[512,512]{1,0:T(8,128)} %copy-done.2, f32[512,512]{1,0:T(8,128)S(1)} %subtract_divide_fusion.2, f32[512,512]{1,0:T(8,128)} %copy-done.16, f32[]{:T(128)} %sqrt.18, f32[]{:T(128)} %bitcast.31, f32[]{:T(128)} %bitcast.30, f32[]{:T(128)} %bitcast.29, f32[512,512]{1,0:T(8,128)S(1)} %copy-done.1, ...), kind=kLoop, calls=%fused_computation.92 | loop fusion | flops 2097152 | bytes 5242900 | tf_op jit(solution)/shard_map/div | solution.py:91
  258.9 3.0 collective-permute-start.12
  263.2 3.0 collective-permute-done.13
  266.4 6.7 %collective-permute-start.14 = (f32[514,1]{1,0:T(8,128)S(1)}, f32[514,1]{1,0:T(8,128)S(1)}, u32[]{:S(2)}, u32[]{:S(2)}) collective-permute-start(f32[514,1]{1,0:T(8,128)S(1)} %get-tuple-element.10), channel_id=1, source_target_pairs={{0,1},{1,2},{2,3},{3,4},{4,5},{5,6},{6,7},{8,9},{9,10},{10,11},{11... | collective-permute-start | bytes 6176 | tf_op jit(solution)/shard_map/ppermute | solution.py:18
  276.4 4.5 %collective-permute-done.15 = f32[514,1]{1,0:T(8,128)S(1)} collective-permute-done((f32[514,1]{1,0:T(8,128)S(1)}, f32[514,1]{1,0:T(8,128)S(1)}, u32[]{:S(2)}, u32[]{:S(2)}) %collective-permute-start.15) | collective-permute-done | bytes 2088 | tf_op jit(solution)/shard_map/ppermute | solution.py:20
  280.9 2.5 convolution_bitcast_fusion
  286.6 37.8 %psum.39 = f32[256]{0:T(256)S(1)} all-reduce(f32[256]{0:T(256)S(1)} %multiply_reduce_fusion), channel_id=1, replica_groups=mesh['gx'=4,'gy'=8] {'gx','gy'}, use_global_device_ids=true, to_apply=%region_8.0 | all-reduce | flops 256 | bytes 2048 | tf_op jit(solution)/shard_map/psum | solution.py:68
  344.7 2.1 multiply_add_fusion
  346.9 2.9 collective-permute-start.16
  351.1 3.0 collective-permute-done.17
  354.3 6.7 %collective-permute-start.18 = (f32[514,1]{1,0:T(8,128)S(1)}, f32[514,1]{1,0:T(8,128)S(1)}, u32[]{:S(2)}, u32[]{:S(2)}) collective-permute-start(f32[514,1]{1,0:T(8,128)S(1)} %get-tuple-element.8), channel_id=1, source_target_pairs={{0,1},{1,2},{2,3},{3,4},{4,5},{5,6},{6,7},{8,9},{9,10},{10,11},{11... | collective-permute-start | bytes 6176 | tf_op jit(solution)/shard_map/ppermute | solution.py:18
  364.3 4.5 %collective-permute-done.19 = f32[514,1]{1,0:T(8,128)S(1)} collective-permute-done((f32[514,1]{1,0:T(8,128)S(1)}, f32[514,1]{1,0:T(8,128)S(1)}, u32[]{:S(2)}, u32[]{:S(2)}) %collective-permute-start.19) | collective-permute-done | bytes 2088 | tf_op jit(solution)/shard_map/ppermute | solution.py:20
  (119 shorter events, 55.8 us)
Async XLA Ops:
  4.0 42.2 %copy-start.1 = (f32[512,512]{1,0:T(8,128)S(1)}, f32[512,512]{1,0:T(8,128)}, u32[]{:S(2)}) copy-start(f32[512,512]{1,0:T(8,128)} %param.5) | copy-start | bytes 3145732
  46.2 22.4 %copy-start.8 = (f32[512,512]{1,0:T(8,128)S(1)}, f32[512,512]{1,0:T(8,128)}, u32[]{:S(2)}) copy-start(f32[512,512]{1,0:T(8,128)} %param.6) | copy-start | bytes 3145732
  46.3 22.3 %copy-start.3 = (f32[512,512]{1,0:T(8,128)S(1)}, f32[512,512]{1,0:T(8,128)}, u32[]{:S(2)}) copy-start(f32[512,512]{1,0:T(8,128)} %param.7) | copy-start | bytes 3145732
  46.3 4.6 %collective-permute-start = (f32[1,512]{1,0:T(1,128)S(1)}, f32[1,512]{1,0:T(1,128)S(1)}, u32[]{:S(2)}, u32[]{:S(2)}) collective-permute-start(f32[1,512]{1,0:T(1,128)S(1)} %get-tuple-element.26), channel_id=1, source_target_pairs={{0,8},{8,16},{16,24},{1,9},{9,17},{17,25},{2,10},{10,18},{18,26},{... | collective-permute-start | bytes 6152 | tf_op jit(solution)/shard_map/ppermute | solution.py:18
  49.6 4.3 %collective-permute-start.1 = (f32[1,512]{1,0:T(1,128)S(1)}, f32[1,512]{1,0:T(1,128)S(1)}, u32[]{:S(2)}, u32[]{:S(2)}) collective-permute-start(f32[1,512]{1,0:T(1,128)S(1)} %get-tuple-element.27), channel_id=1, source_target_pairs={{8,0},{16,8},{24,16},{9,1},{17,9},{25,17},{10,2},{18,10},{26,18},{... | collective-permute-start | bytes 6152 | tf_op jit(solution)/shard_map/ppermute | solution.py:20
  54.1 10.1 %collective-permute-start.2 = (f32[514,1]{1,0:T(8,128)S(1)}, f32[514,1]{1,0:T(8,128)S(1)}, u32[]{:S(2)}, u32[]{:S(2)}) collective-permute-start(f32[514,1]{1,0:T(8,128)S(1)} %get-tuple-element.16), channel_id=1, source_target_pairs={{0,1},{1,2},{2,3},{3,4},{4,5},{5,6},{6,7},{8,9},{9,10},{10,11},{11... | collective-permute-start | bytes 6176 | tf_op jit(solution)/shard_map/ppermute | solution.py:18
  60.8 7.8 %collective-permute-start.3 = (f32[514,1]{1,0:T(8,128)S(1)}, f32[514,1]{1,0:T(8,128)S(1)}, u32[]{:S(2)}, u32[]{:S(2)}) collective-permute-start(f32[514,1]{1,0:T(8,128)S(1)} %get-tuple-element.17), channel_id=1, source_target_pairs={{1,0},{2,1},{3,2},{4,3},{5,4},{6,5},{7,6},{9,8},{10,9},{11,10},{12... | collective-permute-start | bytes 6176 | tf_op jit(solution)/shard_map/ppermute | solution.py:20
  112.7 23.6 %copy-start.9 = (f32[512,512]{1,0:T(8,128)S(1)}, f32[512,512]{1,0:T(8,128)}, u32[]{:S(2)}) copy-start(f32[512,512]{1,0:T(8,128)} %param.6) | copy-start | bytes 3145732
  115.0 4.4 %collective-permute-start.4 = (f32[1,512]{1,0:T(1,128)S(1)}, f32[1,512]{1,0:T(1,128)S(1)}, u32[]{:S(2)}, u32[]{:S(2)}) collective-permute-start(f32[1,512]{1,0:T(1,128)S(1)} %get-tuple-element.24), channel_id=1, source_target_pairs={{0,8},{8,16},{16,24},{1,9},{9,17},{17,25},{2,10},{10,18},{18,26},{... | collective-permute-start | bytes 6152 | tf_op jit(solution)/shard_map/ppermute | solution.py:18
  117.4 4.3 %collective-permute-start.5 = (f32[1,512]{1,0:T(1,128)S(1)}, f32[1,512]{1,0:T(1,128)S(1)}, u32[]{:S(2)}, u32[]{:S(2)}) collective-permute-start(f32[1,512]{1,0:T(1,128)S(1)} %get-tuple-element.25), channel_id=1, source_target_pairs={{8,0},{16,8},{24,16},{9,1},{17,9},{25,17},{10,2},{18,10},{26,18},{... | collective-permute-start | bytes 6152 | tf_op jit(solution)/shard_map/ppermute | solution.py:20
  121.8 10.1 %collective-permute-start.6 = (f32[514,1]{1,0:T(8,128)S(1)}, f32[514,1]{1,0:T(8,128)S(1)}, u32[]{:S(2)}, u32[]{:S(2)}) collective-permute-start(f32[514,1]{1,0:T(8,128)S(1)} %get-tuple-element.14), channel_id=1, source_target_pairs={{0,1},{1,2},{2,3},{3,4},{4,5},{5,6},{6,7},{8,9},{9,10},{10,11},{11... | collective-permute-start | bytes 6176 | tf_op jit(solution)/shard_map/ppermute | solution.py:18
  128.6 7.8 %collective-permute-start.7 = (f32[514,1]{1,0:T(8,128)S(1)}, f32[514,1]{1,0:T(8,128)S(1)}, u32[]{:S(2)}, u32[]{:S(2)}) collective-permute-start(f32[514,1]{1,0:T(8,128)S(1)} %get-tuple-element.15), channel_id=1, source_target_pairs={{1,0},{2,1},{3,2},{4,3},{5,4},{6,5},{7,6},{9,8},{10,9},{11,10},{12... | collective-permute-start | bytes 6176 | tf_op jit(solution)/shard_map/ppermute | solution.py:20
  183.1 25.1 %copy-start.10 = (f32[512,512]{1,0:T(8,128)S(1)}, f32[512,512]{1,0:T(8,128)}, u32[]{:S(2)}) copy-start(f32[512,512]{1,0:T(8,128)} %param.6) | copy-start | bytes 3145732
  186.0 23.0 %copy-start.2 = (f32[512,512]{1,0:T(8,128)}, f32[512,512]{1,0:T(8,128)S(1)}, u32[]{:S(2)}) copy-start(f32[512,512]{1,0:T(8,128)S(1)} %subtract_divide_fusion.1) | copy-start | bytes 3145732
  186.0 22.1 %copy-start.5 = (f32[512,512]{1,0:T(8,128)S(1)}, f32[512,512]{1,0:T(8,128)}, u32[]{:S(2)}) copy-start(f32[512,512]{1,0:T(8,128)} %param.7) | copy-start | bytes 3145732
  186.0 4.4 %collective-permute-start.8 = (f32[1,512]{1,0:T(1,128)S(1)}, f32[1,512]{1,0:T(1,128)S(1)}, u32[]{:S(2)}, u32[]{:S(2)}) collective-permute-start(f32[1,512]{1,0:T(1,128)S(1)} %get-tuple-element.22), channel_id=1, source_target_pairs={{0,8},{8,16},{16,24},{1,9},{9,17},{17,25},{2,10},{10,18},{18,26},{... | collective-permute-start | bytes 6152 | tf_op jit(solution)/shard_map/ppermute | solution.py:18
  189.1 4.3 %collective-permute-start.9 = (f32[1,512]{1,0:T(1,128)S(1)}, f32[1,512]{1,0:T(1,128)S(1)}, u32[]{:S(2)}, u32[]{:S(2)}) collective-permute-start(f32[1,512]{1,0:T(1,128)S(1)} %get-tuple-element.23), channel_id=1, source_target_pairs={{8,0},{16,8},{24,16},{9,1},{17,9},{25,17},{10,2},{18,10},{26,18},{... | collective-permute-start | bytes 6152 | tf_op jit(solution)/shard_map/ppermute | solution.py:20
  193.6 10.1 %collective-permute-start.10 = (f32[514,1]{1,0:T(8,128)S(1)}, f32[514,1]{1,0:T(8,128)S(1)}, u32[]{:S(2)}, u32[]{:S(2)}) collective-permute-start(f32[514,1]{1,0:T(8,128)S(1)} %get-tuple-element.12), channel_id=1, source_target_pairs={{0,1},{1,2},{2,3},{3,4},{4,5},{5,6},{6,7},{8,9},{9,10},{10,11},{11... | collective-permute-start | bytes 6176 | tf_op jit(solution)/shard_map/ppermute | solution.py:18
  200.3 7.8 %collective-permute-start.11 = (f32[514,1]{1,0:T(8,128)S(1)}, f32[514,1]{1,0:T(8,128)S(1)}, u32[]{:S(2)}, u32[]{:S(2)}) collective-permute-start(f32[514,1]{1,0:T(8,128)S(1)} %get-tuple-element.13), channel_id=1, source_target_pairs={{1,0},{2,1},{3,2},{4,3},{5,4},{6,5},{7,6},{9,8},{10,9},{11,10},{12... | collective-permute-start | bytes 6176 | tf_op jit(solution)/shard_map/ppermute | solution.py:20
  254.9 26.0 %copy-start.11 = (f32[512,512]{1,0:T(8,128)S(1)}, f32[512,512]{1,0:T(8,128)}, u32[]{:S(2)}) copy-start(f32[512,512]{1,0:T(8,128)} %param.6) | copy-start | bytes 3145732
  258.8 22.0 %copy-start.14 = (f32[512,512]{1,0:T(8,128)}, f32[512,512]{1,0:T(8,128)S(1)}, u32[]{:S(2)}) copy-start(f32[512,512]{1,0:T(8,128)S(1)} %subtract_divide_fusion) | copy-start | bytes 3145732
  258.9 22.0 %copy-start.6 = (f32[512,512]{1,0:T(8,128)S(1)}, f32[512,512]{1,0:T(8,128)}, u32[]{:S(2)}) copy-start(f32[512,512]{1,0:T(8,128)} %param.7) | copy-start | bytes 3145732
  258.9 4.3 %collective-permute-start.12 = (f32[1,512]{1,0:T(1,128)S(1)}, f32[1,512]{1,0:T(1,128)S(1)}, u32[]{:S(2)}, u32[]{:S(2)}) collective-permute-start(f32[1,512]{1,0:T(1,128)S(1)} %get-tuple-element.20), channel_id=1, source_target_pairs={{0,8},{8,16},{16,24},{1,9},{9,17},{17,25},{2,10},{10,18},{18,26},{... | collective-permute-start | bytes 6152 | tf_op jit(solution)/shard_map/ppermute | solution.py:18
  261.9 4.3 %collective-permute-start.13 = (f32[1,512]{1,0:T(1,128)S(1)}, f32[1,512]{1,0:T(1,128)S(1)}, u32[]{:S(2)}, u32[]{:S(2)}) collective-permute-start(f32[1,512]{1,0:T(1,128)S(1)} %get-tuple-element.21), channel_id=1, source_target_pairs={{8,0},{16,8},{24,16},{9,1},{17,9},{25,17},{10,2},{18,10},{26,18},{... | collective-permute-start | bytes 6152 | tf_op jit(solution)/shard_map/ppermute | solution.py:20
  266.4 10.1 %collective-permute-start.14 = (f32[514,1]{1,0:T(8,128)S(1)}, f32[514,1]{1,0:T(8,128)S(1)}, u32[]{:S(2)}, u32[]{:S(2)}) collective-permute-start(f32[514,1]{1,0:T(8,128)S(1)} %get-tuple-element.10), channel_id=1, source_target_pairs={{0,1},{1,2},{2,3},{3,4},{4,5},{5,6},{6,7},{8,9},{9,10},{10,11},{11... | collective-permute-start | bytes 6176 | tf_op jit(solution)/shard_map/ppermute | solution.py:18
  273.1 7.8 %collective-permute-start.15 = (f32[514,1]{1,0:T(8,128)S(1)}, f32[514,1]{1,0:T(8,128)S(1)}, u32[]{:S(2)}, u32[]{:S(2)}) collective-permute-start(f32[514,1]{1,0:T(8,128)S(1)} %get-tuple-element.11), channel_id=1, source_target_pairs={{1,0},{2,1},{3,2},{4,3},{5,4},{6,5},{7,6},{9,8},{10,9},{11,10},{12... | collective-permute-start | bytes 6176 | tf_op jit(solution)/shard_map/ppermute | solution.py:20
  344.7 24.1 %copy-start.12 = (f32[512,512]{1,0:T(8,128)S(1)}, f32[512,512]{1,0:T(8,128)}, u32[]{:S(2)}) copy-start(f32[512,512]{1,0:T(8,128)} %param.6) | copy-start | bytes 3145732
  346.8 23.9 %copy-start.15 = (f32[512,512]{1,0:T(8,128)}, f32[512,512]{1,0:T(8,128)S(1)}, u32[]{:S(2)}) copy-start(f32[512,512]{1,0:T(8,128)S(1)} %multiply_add_fusion) | copy-start | bytes 3145732
  346.9 4.2 %collective-permute-start.16 = (f32[1,512]{1,0:T(1,128)S(1)}, f32[1,512]{1,0:T(1,128)S(1)}, u32[]{:S(2)}, u32[]{:S(2)}) collective-permute-start(f32[1,512]{1,0:T(1,128)S(1)} %get-tuple-element.18), channel_id=1, source_target_pairs={{0,8},{8,16},{16,24},{1,9},{9,17},{17,25},{2,10},{10,18},{18,26},{... | collective-permute-start | bytes 6152 | tf_op jit(solution)/shard_map/ppermute | solution.py:18
  349.8 4.3 %collective-permute-start.17 = (f32[1,512]{1,0:T(1,128)S(1)}, f32[1,512]{1,0:T(1,128)S(1)}, u32[]{:S(2)}, u32[]{:S(2)}) collective-permute-start(f32[1,512]{1,0:T(1,128)S(1)} %get-tuple-element.19), channel_id=1, source_target_pairs={{8,0},{16,8},{24,16},{9,1},{17,9},{25,17},{10,2},{18,10},{26,18},{... | collective-permute-start | bytes 6152 | tf_op jit(solution)/shard_map/ppermute | solution.py:20
  354.3 10.1 %collective-permute-start.18 = (f32[514,1]{1,0:T(8,128)S(1)}, f32[514,1]{1,0:T(8,128)S(1)}, u32[]{:S(2)}, u32[]{:S(2)}) collective-permute-start(f32[514,1]{1,0:T(8,128)S(1)} %get-tuple-element.8), channel_id=1, source_target_pairs={{0,1},{1,2},{2,3},{3,4},{4,5},{5,6},{6,7},{8,9},{9,10},{10,11},{11... | collective-permute-start | bytes 6176 | tf_op jit(solution)/shard_map/ppermute | solution.py:18
  361.0 7.8 %collective-permute-start.19 = (f32[514,1]{1,0:T(8,128)S(1)}, f32[514,1]{1,0:T(8,128)S(1)}, u32[]{:S(2)}, u32[]{:S(2)}) collective-permute-start(f32[514,1]{1,0:T(8,128)S(1)} %get-tuple-element.9), channel_id=1, source_target_pairs={{1,0},{2,1},{3,2},{4,3},{5,4},{6,5},{7,6},{9,8},{10,9},{11,10},{12... | collective-permute-start | bytes 6176 | tf_op jit(solution)/shard_map/ppermute | solution.py:20
  (7 other events, 49.9 us)
where the time goes:
time: 372 us; the launch traced here: 371 us
  blocking collectives  192 us (52%)
  starting transfers between devices  64.4 us (17%)
  waiting for transfers between devices  42.7 us (11%)
  other arithmetic  28.1 us (8%)
  between operations  19.8 us (5%)
  local copies, waits for them, and re-layouts  13.1 us (4%)
  matrix products  10.4 us (3%)
    psum x5, blocking collectives, sketch(): return lax.psum(partial_value, ('gx', 'gy'))  192 us
    ppermute x10, starting transfers between devices, padded_2(): lax.ppermute(tail, axis, [(i, (i + 1) % count) for i in range(ends)])  48.2 us
    ppermute x10, waiting for transfers between devices, padded_2(): lax.ppermute(head, axis, [((i + 1) % count, i) for i in range(ends)])  36.7 us
    ppermute x10, starting transfers between devices, padded_2(): lax.ppermute(head, axis, [((i + 1) % count, i) for i in range(ends)])  16.2 us
    unnamed x43, local copies, waits for them, and re-layouts  10.5 us
    dot_general x5, matrix products, sketch(): product = jnp.dot(field, sketch_cols.T, precision=lax.Precision.HIGHEST)  9.45 us
    div x3, other arithmetic, body(): basis_vectors.append(remainder / new_norm)  9.05 us
  transfers between devices with their start and end apart: 20, of which 15 were waited for; matrix products, arithmetic and copies ran while one was open for 0% of the time, Pallas kernels for 0%

commit v1 on v0

--- a/solution.py
+++ b/solution.py
@@ -65,7 +65,7 @@
         partial_value = jnp.einsum(
             "ki,ik->k", sketch_rows, product, precision=lax.Precision.HIGHEST
         )
-        return lax.psum(partial_value, ("gx", "gy"))
+        return lax.psum(lax.psum(partial_value, "gy"), "gx")
 
     first_sketch = sketch(right_side)
     beta_norm = jnp.sqrt(jnp.sum(first_sketch * first_sketch))

time: 372 us -> 287 us (0.77)
  blocking collectives: 192 us -> 91.2 us
  waiting for transfers between devices: 42.7 us -> 54 us
  starting transfers between devices: 64.4 us -> 68.4 us
    psum x5 -> x10, blocking collectives: 192 us -> 91.2 us  [sketch(): return lax.psum(lax.psum(partial_value, 'gy'), 'gx')]
    ppermute x10, waiting for transfers between devices: 36.7 us -> 48.7 us  [padded_2(): lax.ppermute(head, axis, [((i + 1) % count, i) for i in range(ends)])]
  transfers between devices with their start and end apart: 20 -> 20, of which waited for: 15 -> 15; matrix products, arithmetic and copies ran while one was open for 0% -> 1% of each run, Pallas kernels for 0% -> 0%
where the time goes in v1:
time: 287 us; the launch traced here: 285 us
  blocking collectives  91.2 us (32%)
  starting transfers between devices  68.4 us (24%)
  waiting for transfers between devices  54 us (19%)
  other arithmetic  28 us (10%)
  between operations  19.9 us (7%)
  local copies, waits for them, and re-layouts  13.2 us (5%)
  matrix products  10.4 us (4%)
    psum x10, blocking collectives, sketch(): return lax.psum(lax.psum(partial_value, 'gy'), 'gx')  91.2 us
    ppermute x10, starting transfers between devices, padded_2(): lax.ppermute(tail, axis, [(i, (i + 1) % count) for i in range(ends)])  51.4 us
    ppermute x10, waiting for transfers between devices, padded_2(): lax.ppermute(head, axis, [((i + 1) % count, i) for i in range(ends)])  48.7 us
    ppermute x10, starting transfers between devices, padded_2(): lax.ppermute(head, axis, [((i + 1) % count, i) for i in range(ends)])  17 us
    unnamed x43, local copies, waits for them, and re-layouts  10.6 us
    dot_general x5, matrix products, sketch(): product = jnp.dot(field, sketch_cols.T, precision=lax.Precision.HIGHEST)  9.44 us
    div x3, other arithmetic, body(): basis_vectors.append(remainder / new_norm)  9.1 us
  transfers between devices with their start and end apart: 20, of which 15 were waited for; matrix products, arithmetic and copies ran while one was open for 1% of the time, Pallas kernels for 0%

profile of v1, /device:TPU:1, one launch (start us, length us, event | category | flops | bytes accessed | tf_op | source)
XLA Modules:
  0.0 285.2 jit_solution(1362355741394492905)
XLA Ops:
  4.3 12.6 %psum.70 = f32[256]{0:T(256)S(1)} all-reduce(f32[256]{0:T(256)S(1)} %multiply_reduce_fusion.4), channel_id=1, replica_groups=mesh['gx'=4,'gy'=8] {'gy'}, use_global_device_ids=true, to_apply=%region_0.0 | all-reduce | flops 256 | bytes 2048 | tf_op jit(solution)/shard_map/psum | solution.py:68
  16.9 10.0 %psum.71 = f32[256]{0:T(256)S(1)} all-reduce(f32[256]{0:T(256)S(1)} %psum.70), channel_id=1, replica_groups=mesh['gx'=4,'gy'=8] {'gx'}, use_global_device_ids=true, to_apply=%region_1.0 | all-reduce | flops 256 | bytes 2048 | tf_op jit(solution)/shard_map/psum | solution.py:68
  31.1 3.0 %collective-permute-done.1 = f32[1,512]{1,0:T(1,128)S(1)} collective-permute-done((f32[1,512]{1,0:T(1,128)S(1)}, f32[1,512]{1,0:T(1,128)S(1)}, u32[]{:S(2)}, u32[]{:S(2)}) %collective-permute-start.1) | collective-permute-done | bytes 2080 | tf_op jit(solution)/shard_map/ppermute | solution.py:20
  34.3 6.1 %collective-permute-start.2 = (f32[514,1]{1,0:T(8,128)S(1)}, f32[514,1]{1,0:T(8,128)S(1)}, u32[]{:S(2)}, u32[]{:S(2)}) collective-permute-start(f32[514,1]{1,0:T(8,128)S(1)} %get-tuple-element.16), channel_id=1, source_target_pairs={{0,1},{1,2},{2,3},{3,4},{4,5},{5,6},{6,7},{8,9},{9,10},{10,11},{11... | collective-permute-start | bytes 6176 | tf_op jit(solution)/shard_map/ppermute | solution.py:18
  40.4 2.8 collective-permute-start.3
  43.7 6.1 %collective-permute-done.3 = f32[514,1]{1,0:T(8,128)S(1)} collective-permute-done((f32[514,1]{1,0:T(8,128)S(1)}, f32[514,1]{1,0:T(8,128)S(1)}, u32[]{:S(2)}, u32[]{:S(2)}) %collective-permute-start.3) | collective-permute-done | bytes 2088 | tf_op jit(solution)/shard_map/ppermute | solution.py:20
  53.0 10.4 %psum.72 = f32[256]{0:T(256)S(1)} all-reduce(f32[256]{0:T(256)S(1)} %multiply_reduce_fusion.3), channel_id=1, replica_groups=mesh['gx'=4,'gy'=8] {'gy'}, use_global_device_ids=true, to_apply=%region_3.0 | all-reduce | flops 256 | bytes 2048 | tf_op jit(solution)/shard_map/psum | solution.py:68
  63.4 7.1 %psum.73 = f32[256]{0:T(256)S(1)} all-reduce(f32[256]{0:T(256)S(1)} %psum.72), channel_id=1, replica_groups=mesh['gx'=4,'gy'=8] {'gx'}, use_global_device_ids=true, to_apply=%region_4.0 | all-reduce | flops 256 | bytes 2048 | tf_op jit(solution)/shard_map/psum | solution.py:68
  75.4 2.9 %collective-permute-start.4 = (f32[1,512]{1,0:T(1,128)S(1)}, f32[1,512]{1,0:T(1,128)S(1)}, u32[]{:S(2)}, u32[]{:S(2)}) collective-permute-start(f32[1,512]{1,0:T(1,128)S(1)} %get-tuple-element.24), channel_id=1, source_target_pairs={{0,8},{8,16},{16,24},{1,9},{9,17},{17,25},{2,10},{10,18},{18,26},{... | collective-permute-start | bytes 6152 | tf_op jit(solution)/shard_map/ppermute | solution.py:18
  82.9 7.7 %collective-permute-start.6 = (f32[514,1]{1,0:T(8,128)S(1)}, f32[514,1]{1,0:T(8,128)S(1)}, u32[]{:S(2)}, u32[]{:S(2)}) collective-permute-start(f32[514,1]{1,0:T(8,128)S(1)} %get-tuple-element.14), channel_id=1, source_target_pairs={{0,1},{1,2},{2,3},{3,4},{4,5},{5,6},{6,7},{8,9},{9,10},{10,11},{11... | collective-permute-start | bytes 6176 | tf_op jit(solution)/shard_map/ppermute | solution.py:18
  93.9 7.1 %collective-permute-done.7 = f32[514,1]{1,0:T(8,128)S(1)} collective-permute-done((f32[514,1]{1,0:T(8,128)S(1)}, f32[514,1]{1,0:T(8,128)S(1)}, u32[]{:S(2)}, u32[]{:S(2)}) %collective-permute-start.7) | collective-permute-done | bytes 2088 | tf_op jit(solution)/shard_map/ppermute | solution.py:20
  107.7 10.4 %psum.74 = f32[256]{0:T(256)S(1)} all-reduce(f32[256]{0:T(256)S(1)} %multiply_reduce_fusion.2), channel_id=1, replica_groups=mesh['gx'=4,'gy'=8] {'gy'}, use_global_device_ids=true, to_apply=%region_6.0 | all-reduce | flops 256 | bytes 2048 | tf_op jit(solution)/shard_map/psum | solution.py:68
  118.1 6.6 %psum.75 = f32[256]{0:T(256)S(1)} all-reduce(f32[256]{0:T(256)S(1)} %psum.74), channel_id=1, replica_groups=mesh['gx'=4,'gy'=8] {'gx'}, use_global_device_ids=true, to_apply=%region_7.0 | all-reduce | flops 256 | bytes 2048 | tf_op jit(solution)/shard_map/psum | solution.py:68
  126.9 2.9 %subtract_divide_fusion.1 = f32[512,512]{1,0:T(8,128)S(1)} fusion(f32[512,512]{1,0:T(8,128)S(1)} %subtract_divide_fusion.2, f32[512,512]{1,0:T(8,128)} %copy-done.18, f32[]{:T(128)} %sqrt.17, f32[]{:T(128)} %bitcast.20, f32[]{:T(128)} %bitcast.19, f32[512,512]{1,0:T(8,128)S(1)} %copy-done.1, f32[]{:T(128)S(6)} %sqrt.15), kind=kLoop, calls=%fused_computation.93 | loop fusion | flops 1572864 | bytes 4194320 | tf_op jit(solution)/shard_map/div | solution.py:91
  129.9 3.4 %collective-permute-start.8 = (f32[1,512]{1,0:T(1,128)S(1)}, f32[1,512]{1,0:T(1,128)S(1)}, u32[]{:S(2)}, u32[]{:S(2)}) collective-permute-start(f32[1,512]{1,0:T(1,128)S(1)} %get-tuple-element.22), channel_id=1, source_target_pairs={{0,8},{8,16},{16,24},{1,9},{9,17},{17,25},{2,10},{10,18},{18,26},{... | collective-permute-start | bytes 6152 | tf_op jit(solution)/shard_map/ppermute | solution.py:18
  134.7 3.0 %collective-permute-done.9 = f32[1,512]{1,0:T(1,128)S(1)} collective-permute-done((f32[1,512]{1,0:T(1,128)S(1)}, f32[1,512]{1,0:T(1,128)S(1)}, u32[]{:S(2)}, u32[]{:S(2)}) %collective-permute-start.9) | collective-permute-done | bytes 2080 | tf_op jit(solution)/shard_map/ppermute | solution.py:20
  137.8 7.7 %collective-permute-start.10 = (f32[514,1]{1,0:T(8,128)S(1)}, f32[514,1]{1,0:T(8,128)S(1)}, u32[]{:S(2)}, u32[]{:S(2)}) collective-permute-start(f32[514,1]{1,0:T(8,128)S(1)} %get-tuple-element.12), channel_id=1, source_target_pairs={{0,1},{1,2},{2,3},{3,4},{4,5},{5,6},{6,7},{8,9},{9,10},{10,11},{11... | collective-permute-start | bytes 6176 | tf_op jit(solution)/shard_map/ppermute | solution.py:18
  148.8 7.1 %collective-permute-done.11 = f32[514,1]{1,0:T(8,128)S(1)} collective-permute-done((f32[514,1]{1,0:T(8,128)S(1)}, f32[514,1]{1,0:T(8,128)S(1)}, u32[]{:S(2)}, u32[]{:S(2)}) %collective-permute-start.11) | collective-permute-done | bytes 2088 | tf_op jit(solution)/shard_map/ppermute | solution.py:20
  162.8 10.4 %psum.76 = f32[256]{0:T(256)S(1)} all-reduce(f32[256]{0:T(256)S(1)} %multiply_reduce_fusion.1), channel_id=1, replica_groups=mesh['gx'=4,'gy'=8] {'gy'}, use_global_device_ids=true, to_apply=%region_9.0 | all-reduce | flops 256 | bytes 2048 | tf_op jit(solution)/shard_map/psum | solution.py:68
  173.1 6.8 %psum.77 = f32[256]{0:T(256)S(1)} all-reduce(f32[256]{0:T(256)S(1)} %psum.76), channel_id=1, replica_groups=mesh['gx'=4,'gy'=8] {'gx'}, use_global_device_ids=true, to_apply=%region_10.0 | all-reduce | flops 256 | bytes 2048 | tf_op jit(solution)/shard_map/psum | solution.py:68
  182.1 4.0 %subtract_divide_fusion = f32[512,512]{1,0:T(8,128)S(1)} fusion(f32[512,512]{1,0:T(8,128)} %copy-done.2, f32[512,512]{1,0:T(8,128)S(1)} %subtract_divide_fusion.2, f32[512,512]{1,0:T(8,128)} %copy-done.16, f32[]{:T(128)} %sqrt.18, f32[]{:T(128)} %bitcast.31, f32[]{:T(128)} %bitcast.30, f32[]{:T(128)} %bitcast.29, f32[512,512]{1,0:T(8,128)S(1)} %copy-done.1, ...), kind=kLoop, calls=%fused_computation.92 | loop fusion | flops 2097152 | bytes 5242900 | tf_op jit(solution)/shard_map/div | solution.py:91
  186.1 3.4 %collective-permute-start.12 = (f32[1,512]{1,0:T(1,128)S(1)}, f32[1,512]{1,0:T(1,128)S(1)}, u32[]{:S(2)}, u32[]{:S(2)}) collective-permute-start(f32[1,512]{1,0:T(1,128)S(1)} %get-tuple-element.20), channel_id=1, source_target_pairs={{0,8},{8,16},{16,24},{1,9},{9,17},{17,25},{2,10},{10,18},{18,26},{... | collective-permute-start | bytes 6152 | tf_op jit(solution)/shard_map/ppermute | solution.py:18
  190.9 3.0 %collective-permute-done.13 = f32[1,512]{1,0:T(1,128)S(1)} collective-permute-done((f32[1,512]{1,0:T(1,128)S(1)}, f32[1,512]{1,0:T(1,128)S(1)}, u32[]{:S(2)}, u32[]{:S(2)}) %collective-permute-start.13) | collective-permute-done | bytes 2080 | tf_op jit(solution)/shard_map/ppermute | solution.py:20
  194.0 7.7 %collective-permute-start.14 = (f32[514,1]{1,0:T(8,128)S(1)}, f32[514,1]{1,0:T(8,128)S(1)}, u32[]{:S(2)}, u32[]{:S(2)}) collective-permute-start(f32[514,1]{1,0:T(8,128)S(1)} %get-tuple-element.10), channel_id=1, source_target_pairs={{0,1},{1,2},{2,3},{3,4},{4,5},{5,6},{6,7},{8,9},{9,10},{10,11},{11... | collective-permute-start | bytes 6176 | tf_op jit(solution)/shard_map/ppermute | solution.py:18
  205.0 7.1 %collective-permute-done.15 = f32[514,1]{1,0:T(8,128)S(1)} collective-permute-done((f32[514,1]{1,0:T(8,128)S(1)}, f32[514,1]{1,0:T(8,128)S(1)}, u32[]{:S(2)}, u32[]{:S(2)}) %collective-permute-start.15) | collective-permute-done | bytes 2088 | tf_op jit(solution)/shard_map/ppermute | solution.py:20
  212.1 2.5 convolution_bitcast_fusion
  217.8 10.4 %psum.78 = f32[256]{0:T(256)S(1)} all-reduce(f32[256]{0:T(256)S(1)} %multiply_reduce_fusion), channel_id=1, replica_groups=mesh['gx'=4,'gy'=8] {'gy'}, use_global_device_ids=true, to_apply=%region_12.0 | all-reduce | flops 256 | bytes 2048 | tf_op jit(solution)/shard_map/psum | solution.py:68
  228.2 6.6 %psum.79 = f32[256]{0:T(256)S(1)} all-reduce(f32[256]{0:T(256)S(1)} %psum.78), channel_id=1, replica_groups=mesh['gx'=4,'gy'=8] {'gx'}, use_global_device_ids=true, to_apply=%region_13.0 | all-reduce | flops 256 | bytes 2048 | tf_op jit(solution)/shard_map/psum | solution.py:68
  257.3 3.4 %collective-permute-start.16 = (f32[1,512]{1,0:T(1,128)S(1)}, f32[1,512]{1,0:T(1,128)S(1)}, u32[]{:S(2)}, u32[]{:S(2)}) collective-permute-start(f32[1,512]{1,0:T(1,128)S(1)} %get-tuple-element.18), channel_id=1, source_target_pairs={{0,8},{8,16},{16,24},{1,9},{9,17},{17,25},{2,10},{10,18},{18,26},{... | collective-permute-start | bytes 6152 | tf_op jit(solution)/shard_map/ppermute | solution.py:18
  262.0 3.0 %collective-permute-done.17 = f32[1,512]{1,0:T(1,128)S(1)} collective-permute-done((f32[1,512]{1,0:T(1,128)S(1)}, f32[1,512]{1,0:T(1,128)S(1)}, u32[]{:S(2)}, u32[]{:S(2)}) %collective-permute-start.17) | collective-permute-done | bytes 2080 | tf_op jit(solution)/shard_map/ppermute | solution.py:20
  265.2 7.7 %collective-permute-start.18 = (f32[514,1]{1,0:T(8,128)S(1)}, f32[514,1]{1,0:T(8,128)S(1)}, u32[]{:S(2)}, u32[]{:S(2)}) collective-permute-start(f32[514,1]{1,0:T(8,128)S(1)} %get-tuple-element.8), channel_id=1, source_target_pairs={{0,1},{1,2},{2,3},{3,4},{4,5},{5,6},{6,7},{8,9},{9,10},{10,11},{11... | collective-permute-start | bytes 6176 | tf_op jit(solution)/shard_map/ppermute | solution.py:18
  276.2 7.1 %collective-permute-done.19 = f32[514,1]{1,0:T(8,128)S(1)} collective-permute-done((f32[514,1]{1,0:T(8,128)S(1)}, f32[514,1]{1,0:T(8,128)S(1)}, u32[]{:S(2)}, u32[]{:S(2)}) %collective-permute-start.19) | collective-permute-done | bytes 2088 | tf_op jit(solution)/shard_map/ppermute | solution.py:20
  (124 shorter events, 65.4 us)
Async XLA Ops:
  4.0 24.2 %copy-start.1 = (f32[512,512]{1,0:T(8,128)S(1)}, f32[512,512]{1,0:T(8,128)}, u32[]{:S(2)}) copy-start(f32[512,512]{1,0:T(8,128)} %param.5) | copy-start | bytes 3145732
  28.4 2.7 collective-permute-start
  29.8 4.3 %collective-permute-start.1 = (f32[1,512]{1,0:T(1,128)S(1)}, f32[1,512]{1,0:T(1,128)S(1)}, u32[]{:S(2)}, u32[]{:S(2)}) collective-permute-start(f32[1,512]{1,0:T(1,128)S(1)} %get-tuple-element.27), channel_id=1, source_target_pairs={{8,0},{16,8},{24,16},{9,1},{17,9},{25,17},{10,2},{18,10},{26,18},{... | collective-permute-start | bytes 6152 | tf_op jit(solution)/shard_map/ppermute | solution.py:20
  34.3 9.4 %collective-permute-start.2 = (f32[514,1]{1,0:T(8,128)S(1)}, f32[514,1]{1,0:T(8,128)S(1)}, u32[]{:S(2)}, u32[]{:S(2)}) collective-permute-start(f32[514,1]{1,0:T(8,128)S(1)} %get-tuple-element.16), channel_id=1, source_target_pairs={{0,1},{1,2},{2,3},{3,4},{4,5},{5,6},{6,7},{8,9},{9,10},{10,11},{11... | collective-permute-start | bytes 6176 | tf_op jit(solution)/shard_map/ppermute | solution.py:18
  40.4 9.5 %collective-permute-start.3 = (f32[514,1]{1,0:T(8,128)S(1)}, f32[514,1]{1,0:T(8,128)S(1)}, u32[]{:S(2)}, u32[]{:S(2)}) collective-permute-start(f32[514,1]{1,0:T(8,128)S(1)} %get-tuple-element.17), channel_id=1, source_target_pairs={{1,0},{2,1},{3,2},{4,3},{5,4},{6,5},{7,6},{9,8},{10,9},{11,10},{12... | collective-permute-start | bytes 6176 | tf_op jit(solution)/shard_map/ppermute | solution.py:20
  73.2 27.7 %copy-start.9 = (f32[512,512]{1,0:T(8,128)S(1)}, f32[512,512]{1,0:T(8,128)}, u32[]{:S(2)}) copy-start(f32[512,512]{1,0:T(8,128)} %param.6) | copy-start | bytes 3145732
  75.4 25.5 %copy-start.4 = (f32[512,512]{1,0:T(8,128)S(1)}, f32[512,512]{1,0:T(8,128)}, u32[]{:S(2)}) copy-start(f32[512,512]{1,0:T(8,128)} %param.7) | copy-start | bytes 3145732
  75.4 4.9 %collective-permute-start.4 = (f32[1,512]{1,0:T(1,128)S(1)}, f32[1,512]{1,0:T(1,128)S(1)}, u32[]{:S(2)}, u32[]{:S(2)}) collective-permute-start(f32[1,512]{1,0:T(1,128)S(1)} %get-tuple-element.24), channel_id=1, source_target_pairs={{0,8},{8,16},{16,24},{1,9},{9,17},{17,25},{2,10},{10,18},{18,26},{... | collective-permute-start | bytes 6152 | tf_op jit(solution)/shard_map/ppermute | solution.py:18
  78.4 4.3 %collective-permute-start.5 = (f32[1,512]{1,0:T(1,128)S(1)}, f32[1,512]{1,0:T(1,128)S(1)}, u32[]{:S(2)}, u32[]{:S(2)}) collective-permute-start(f32[1,512]{1,0:T(1,128)S(1)} %get-tuple-element.25), channel_id=1, source_target_pairs={{8,0},{16,8},{24,16},{9,1},{17,9},{25,17},{10,2},{18,10},{26,18},{... | collective-permute-start | bytes 6152 | tf_op jit(solution)/shard_map/ppermute | solution.py:20
  82.9 11.0 %collective-permute-start.6 = (f32[514,1]{1,0:T(8,128)S(1)}, f32[514,1]{1,0:T(8,128)S(1)}, u32[]{:S(2)}, u32[]{:S(2)}) collective-permute-start(f32[514,1]{1,0:T(8,128)S(1)} %get-tuple-element.14), channel_id=1, source_target_pairs={{0,1},{1,2},{2,3},{3,4},{4,5},{5,6},{6,7},{8,9},{9,10},{10,11},{11... | collective-permute-start | bytes 6176 | tf_op jit(solution)/shard_map/ppermute | solution.py:18
  90.5 10.4 %collective-permute-start.7 = (f32[514,1]{1,0:T(8,128)S(1)}, f32[514,1]{1,0:T(8,128)S(1)}, u32[]{:S(2)}, u32[]{:S(2)}) collective-permute-start(f32[514,1]{1,0:T(8,128)S(1)} %get-tuple-element.15), channel_id=1, source_target_pairs={{1,0},{2,1},{3,2},{4,3},{5,4},{6,5},{7,6},{9,8},{10,9},{11,10},{12... | collective-permute-start | bytes 6176 | tf_op jit(solution)/shard_map/ppermute | solution.py:20
  126.9 29.0 %copy-start.10 = (f32[512,512]{1,0:T(8,128)S(1)}, f32[512,512]{1,0:T(8,128)}, u32[]{:S(2)}) copy-start(f32[512,512]{1,0:T(8,128)} %param.6) | copy-start | bytes 3145732
  129.9 26.9 %copy-start.2 = (f32[512,512]{1,0:T(8,128)}, f32[512,512]{1,0:T(8,128)S(1)}, u32[]{:S(2)}) copy-start(f32[512,512]{1,0:T(8,128)S(1)} %subtract_divide_fusion.1) | copy-start | bytes 3145732
  129.9 26.0 %copy-start.5 = (f32[512,512]{1,0:T(8,128)S(1)}, f32[512,512]{1,0:T(8,128)}, u32[]{:S(2)}) copy-start(f32[512,512]{1,0:T(8,128)} %param.7) | copy-start | bytes 3145732
  129.9 4.8 %collective-permute-start.8 = (f32[1,512]{1,0:T(1,128)S(1)}, f32[1,512]{1,0:T(1,128)S(1)}, u32[]{:S(2)}, u32[]{:S(2)}) collective-permute-start(f32[1,512]{1,0:T(1,128)S(1)} %get-tuple-element.22), channel_id=1, source_target_pairs={{0,8},{8,16},{16,24},{1,9},{9,17},{17,25},{2,10},{10,18},{18,26},{... | collective-permute-start | bytes 6152 | tf_op jit(solution)/shard_map/ppermute | solution.py:18
  133.4 4.3 %collective-permute-start.9 = (f32[1,512]{1,0:T(1,128)S(1)}, f32[1,512]{1,0:T(1,128)S(1)}, u32[]{:S(2)}, u32[]{:S(2)}) collective-permute-start(f32[1,512]{1,0:T(1,128)S(1)} %get-tuple-element.23), channel_id=1, source_target_pairs={{8,0},{16,8},{24,16},{9,1},{17,9},{25,17},{10,2},{18,10},{26,18},{... | collective-permute-start | bytes 6152 | tf_op jit(solution)/shard_map/ppermute | solution.py:20
  137.8 11.0 %collective-permute-start.10 = (f32[514,1]{1,0:T(8,128)S(1)}, f32[514,1]{1,0:T(8,128)S(1)}, u32[]{:S(2)}, u32[]{:S(2)}) collective-permute-start(f32[514,1]{1,0:T(8,128)S(1)} %get-tuple-element.12), channel_id=1, source_target_pairs={{0,1},{1,2},{2,3},{3,4},{4,5},{5,6},{6,7},{8,9},{9,10},{10,11},{11... | collective-permute-start | bytes 6176 | tf_op jit(solution)/shard_map/ppermute | solution.py:18
  145.5 10.4 %collective-permute-start.11 = (f32[514,1]{1,0:T(8,128)S(1)}, f32[514,1]{1,0:T(8,128)S(1)}, u32[]{:S(2)}, u32[]{:S(2)}) collective-permute-start(f32[514,1]{1,0:T(8,128)S(1)} %get-tuple-element.13), channel_id=1, source_target_pairs={{1,0},{2,1},{3,2},{4,3},{5,4},{6,5},{7,6},{9,8},{10,9},{11,10},{12... | collective-permute-start | bytes 6176 | tf_op jit(solution)/shard_map/ppermute | solution.py:20
  182.1 30.0 %copy-start.11 = (f32[512,512]{1,0:T(8,128)S(1)}, f32[512,512]{1,0:T(8,128)}, u32[]{:S(2)}) copy-start(f32[512,512]{1,0:T(8,128)} %param.6) | copy-start | bytes 3145732
  186.0 26.0 %copy-start.14 = (f32[512,512]{1,0:T(8,128)}, f32[512,512]{1,0:T(8,128)S(1)}, u32[]{:S(2)}) copy-start(f32[512,512]{1,0:T(8,128)S(1)} %subtract_divide_fusion) | copy-start | bytes 3145732
  186.1 26.0 %copy-start.6 = (f32[512,512]{1,0:T(8,128)S(1)}, f32[512,512]{1,0:T(8,128)}, u32[]{:S(2)}) copy-start(f32[512,512]{1,0:T(8,128)} %param.7) | copy-start | bytes 3145732
  186.1 4.8 %collective-permute-start.12 = (f32[1,512]{1,0:T(1,128)S(1)}, f32[1,512]{1,0:T(1,128)S(1)}, u32[]{:S(2)}, u32[]{:S(2)}) collective-permute-start(f32[1,512]{1,0:T(1,128)S(1)} %get-tuple-element.20), channel_id=1, source_target_pairs={{0,8},{8,16},{16,24},{1,9},{9,17},{17,25},{2,10},{10,18},{18,26},{... | collective-permute-start | bytes 6152 | tf_op jit(solution)/shard_map/ppermute | solution.py:18
  189.5 4.3 %collective-permute-start.13 = (f32[1,512]{1,0:T(1,128)S(1)}, f32[1,512]{1,0:T(1,128)S(1)}, u32[]{:S(2)}, u32[]{:S(2)}) collective-permute-start(f32[1,512]{1,0:T(1,128)S(1)} %get-tuple-element.21), channel_id=1, source_target_pairs={{8,0},{16,8},{24,16},{9,1},{17,9},{25,17},{10,2},{18,10},{26,18},{... | collective-permute-start | bytes 6152 | tf_op jit(solution)/shard_map/ppermute | solution.py:20
  194.0 11.0 %collective-permute-start.14 = (f32[514,1]{1,0:T(8,128)S(1)}, f32[514,1]{1,0:T(8,128)S(1)}, u32[]{:S(2)}, u32[]{:S(2)}) collective-permute-start(f32[514,1]{1,0:T(8,128)S(1)} %get-tuple-element.10), channel_id=1, source_target_pairs={{0,1},{1,2},{2,3},{3,4},{4,5},{5,6},{6,7},{8,9},{9,10},{10,11},{11... | collective-permute-start | bytes 6176 | tf_op jit(solution)/shard_map/ppermute | solution.py:18
  201.7 10.4 %collective-permute-start.15 = (f32[514,1]{1,0:T(8,128)S(1)}, f32[514,1]{1,0:T(8,128)S(1)}, u32[]{:S(2)}, u32[]{:S(2)}) collective-permute-start(f32[514,1]{1,0:T(8,128)S(1)} %get-tuple-element.11), channel_id=1, source_target_pairs={{1,0},{2,1},{3,2},{4,3},{5,4},{6,5},{7,6},{9,8},{10,9},{11,10},{12... | collective-permute-start | bytes 6176 | tf_op jit(solution)/shard_map/ppermute | solution.py:20
  255.1 28.2 %copy-start.12 = (f32[512,512]{1,0:T(8,128)S(1)}, f32[512,512]{1,0:T(8,128)}, u32[]{:S(2)}) copy-start(f32[512,512]{1,0:T(8,128)} %param.6) | copy-start | bytes 3145732
  257.2 27.9 %copy-start.15 = (f32[512,512]{1,0:T(8,128)}, f32[512,512]{1,0:T(8,128)S(1)}, u32[]{:S(2)}) copy-start(f32[512,512]{1,0:T(8,128)S(1)} %multiply_add_fusion) | copy-start | bytes 3145732
  257.2 26.0 %copy-start.7 = (f32[512,512]{1,0:T(8,128)S(1)}, f32[512,512]{1,0:T(8,128)}, u32[]{:S(2)}) copy-start(f32[512,512]{1,0:T(8,128)} %param.7) | copy-start | bytes 3145732
  257.3 4.8 %collective-permute-start.16 = (f32[1,512]{1,0:T(1,128)S(1)}, f32[1,512]{1,0:T(1,128)S(1)}, u32[]{:S(2)}, u32[]{:S(2)}) collective-permute-start(f32[1,512]{1,0:T(1,128)S(1)} %get-tuple-element.18), channel_id=1, source_target_pairs={{0,8},{8,16},{16,24},{1,9},{9,17},{17,25},{2,10},{10,18},{18,26},{... | collective-permute-start | bytes 6152 | tf_op jit(solution)/shard_map/ppermute | solution.py:18
  260.7 4.3 %collective-permute-start.17 = (f32[1,512]{1,0:T(1,128)S(1)}, f32[1,512]{1,0:T(1,128)S(1)}, u32[]{:S(2)}, u32[]{:S(2)}) collective-permute-start(f32[1,512]{1,0:T(1,128)S(1)} %get-tuple-element.19), channel_id=1, source_target_pairs={{8,0},{16,8},{24,16},{9,1},{17,9},{25,17},{10,2},{18,10},{26,18},{... | collective-permute-start | bytes 6152 | tf_op jit(solution)/shard_map/ppermute | solution.py:20
  265.2 11.0 %collective-permute-start.18 = (f32[514,1]{1,0:T(8,128)S(1)}, f32[514,1]{1,0:T(8,128)S(1)}, u32[]{:S(2)}, u32[]{:S(2)}) collective-permute-start(f32[514,1]{1,0:T(8,128)S(1)} %get-tuple-element.8), channel_id=1, source_target_pairs={{0,1},{1,2},{2,3},{3,4},{4,5},{5,6},{6,7},{8,9},{9,10},{10,11},{11... | collective-permute-start | bytes 6176 | tf_op jit(solution)/shard_map/ppermute | solution.py:18
  272.9 10.4 %collective-permute-start.19 = (f32[514,1]{1,0:T(8,128)S(1)}, f32[514,1]{1,0:T(8,128)S(1)}, u32[]{:S(2)}, u32[]{:S(2)}) collective-permute-start(f32[514,1]{1,0:T(8,128)S(1)} %get-tuple-element.9), channel_id=1, source_target_pairs={{1,0},{2,1},{3,2},{4,3},{5,4},{6,5},{7,6},{9,8},{10,9},{11,10},{12... | collective-permute-start | bytes 6176 | tf_op jit(solution)/shard_map/ppermute | solution.py:20
  (7 other events, 49.6 us)
